TPU v7x, 256 devices: a whole 4x4x8 slice. The times are simulated.
256 devices in a mesh: row: 16 (over z_hi, x), col: 16 (over z_lo, y, core).
Axes of the slice: x: 4, y: 4, z: 8 (z_hi: 4, z_lo: 2; z = z_hi * 2 + z_lo), core: 2. Of those that a mesh axis runs over, the one named last changes fastest.
Arguments:
- signal: bfloat16 [32768, 2048], P('row', 'col'), may hold values from -40 to 40
- norm_gain: float32 [2048], replicated, may hold values from 0.5 to 2
- qkv_weight: bfloat16 [2048, 6144], P('row', 'col'), may hold values from -4 to 4
- out_weight: bfloat16 [2048, 2048], P('row', 'col'), may hold values from -1 to 1
Outputs:
- layer_out: bfloat16 [32768, 2048], P('row', 'col')
All inputs are finite; a program needn't handle non-finite values.
Results may differ from a plain program's by a relative error of at most 0.006.
Values may be sent and summed in bfloat16 or wider, within the bound.
No kernel may reach another device: no remote copies, remote signals or barrier semaphores. Data moves between devices by JAX's collectives and lax.ppermute only.
A program may use at most 64 MiB of HBM per device.

v0:
```python
import math
import jax
import jax.numpy as jnp
from jax import lax
from jax.sharding import PartitionSpec as P

HS = 128
COLS = 1024
EPSILON = 1e-05
NEGATIVE = -1e30


def row_softmax(row_block):
    head_size = row_block.shape[-1] // 3
    queries = row_block[..., :head_size]
    key_part = row_block[..., head_size : 2 * head_size]
    values = row_block[..., 2 * head_size :]
    factor = 1.0 / math.sqrt(head_size)
    scores = (
        jnp.einsum("chd,ehd->hce", queries, key_part, preferred_element_type=jnp.float32) * factor
    )
    length = row_block.shape[0]
    causal = jnp.arange(length)[:, None] >= jnp.arange(length)[None, :]
    scores = jnp.where(causal, scores, NEGATIVE)
    maxima = jnp.max(scores, axis=-1)
    weights = jnp.where(causal, jnp.exp(scores - maxima[..., None]), 0.0)
    totals = jnp.sum(weights, axis=-1)
    summed = jnp.einsum(
        "hce,ehd->chd", weights.astype(jnp.bfloat16), values, preferred_element_type=jnp.float32
    )
    return (summed, maxima.T, totals.T)


def column_softmax(gathered):
    head_size = gathered.shape[-1] // 3
    queries = gathered[..., :head_size]
    key_part = gathered[..., head_size : 2 * head_size]
    values = gathered[..., 2 * head_size :]
    factor = 1.0 / math.sqrt(head_size)
    scores = (
        jnp.einsum("rchd,schd->chrs", queries, key_part, preferred_element_type=jnp.float32)
        * factor
    )
    length = gathered.shape[0]
    earlier = jnp.arange(length)[:, None] > jnp.arange(length)[None, :]
    scores = jnp.where(earlier, scores, NEGATIVE)
    maxima = jnp.max(scores, axis=-1)
    weights = jnp.where(earlier, jnp.exp(scores - maxima[..., None]), 0.0)
    totals = jnp.sum(weights, axis=-1)
    summed = jnp.einsum(
        "chrs,schd->rchd", weights.astype(jnp.bfloat16), values, preferred_element_type=jnp.float32
    )
    maxima_rows = jnp.transpose(maxima, (2, 0, 1))
    totals_rows = jnp.transpose(totals, (2, 0, 1))
    return (
        lax.all_to_all(summed, "row", split_axis=0, concat_axis=1, tiled=True),
        lax.all_to_all(maxima_rows, "row", split_axis=0, concat_axis=1, tiled=True),
        lax.all_to_all(totals_rows, "row", split_axis=0, concat_axis=1, tiled=True),
    )


def per_device(signal, norm_gain, qkv_weight, out_weight):
    samples = signal.shape[0]
    gathered = lax.all_gather(signal, "col", axis=1, tiled=True)
    widened = gathered.astype(jnp.float32)
    average = jnp.mean(widened, axis=1, keepdims=True)
    variance = jnp.mean((widened - average) ** 2, axis=1, keepdims=True)
    normed = ((widened - average) * lax.rsqrt(variance + EPSILON) * norm_gain).astype(jnp.bfloat16)
    qkv_width = qkv_weight.shape[1]
    piece_qkv = lax.all_gather(qkv_weight, "row", axis=0, tiled=True)
    piece_out = lax.all_gather(out_weight, "row", axis=0, tiled=True)
    projected_sum = jnp.dot(normed, piece_qkv, preferred_element_type=jnp.float32)
    qkv = projected_sum.astype(jnp.bfloat16)
    rows_here = samples // COLS
    heads_here = qkv_width // (3 * HS)
    stacked = qkv.reshape(rows_here, COLS, heads_here, 3 * HS)
    row_acc, row_max, row_total = lax.map(row_softmax, stacked)
    col_acc, col_max, col_total = column_softmax(
        lax.all_to_all(stacked, "row", split_axis=1, concat_axis=0, tiled=True)
    )
    highest = jnp.maximum(row_max, col_max)
    row_factor = jnp.exp(row_max - highest)
    col_factor = jnp.exp(col_max - highest)
    denominator = row_factor * row_total + col_factor * col_total
    merged = (row_factor[..., None] * row_acc + col_factor[..., None] * col_acc) / denominator[
        ..., None
    ]
    attended = merged.astype(jnp.bfloat16).reshape(samples, heads_here * HS)
    residual = signal.astype(jnp.float32)
    branch = jnp.dot(
        lax.all_gather(attended, "col", axis=1, tiled=True),
        piece_out,
        preferred_element_type=jnp.float32,
    )
    return (residual + branch).astype(jnp.bfloat16)


def solution(mesh):
    return jax.shard_map(
        per_device,
        mesh=mesh,
        in_specs=(P("row", "col"), P(), P("row", "col"), P("row", "col")),
        out_specs=P("row", "col"),
        check_vma=False,
    )
```

profile of v0, /device:TPU:1, one launch (start us, length us, event | category | flops | bytes accessed | tf_op | source)
XLA Modules:
  0.0 338.2 jit_solution(2449595090421957147)
XLA Ops:
  8.0 69.0 %all-gather.4.cloned.1.call-done = bf16[2048,2048]{1,0:T(8,128)(2,1)} async-done(((bf16[2048,128]{1,0:T(8,128)(2,1)}), bf16[2048,2048]{1,0:T(8,128)(2,1)}) %all-gather.4.cloned.1.call-update) | async-done | bytes 8388624 | tf_op jit(solution)/shard_map/all_gather | solution.py:64
  77.0 4.7 %convert_reduce_fusion = f32[2048]{0:T(1024)S(1)} fusion(bf16[2048,2048]{1,0:T(8,128)(2,1)} %all-gather.4.cloned.1.call-done), kind=kLoop, calls=%fused_computation.18 | loop fusion | flops 8386560 | bytes 8396800 | tf_op jit(solution)/shard_map/reduce_sum | solution.py:66
  81.7 1.1 copy-done.1
  82.8 2.3 fusion.14
  85.1 47.5 %all-gather.6.cloned.1.call-done = bf16[2048,384]{1,0:T(8,128)(2,1)} async-done(((bf16[128,384]{1,0:T(8,128)(2,1)}), bf16[2048,384]{1,0:T(8,128)(2,1)}) %all-gather.6.cloned.1.call-update) | async-done | bytes 1572880 | tf_op jit(solution)/shard_map/all_gather | solution.py:70
  132.6 8.5 %fusion.22 = bf16[2048,384]{1,0:T(8,128)(2,1)S(1)} fusion(bf16[2048,384]{1,0:T(8,128)(2,1)} %all-gather.6.cloned.1.call-done, bf16[2048,2048]{1,0:T(8,128)(2,1)} %all-gather.4.cloned.1.call-done, f32[2048]{0:T(1024)S(1)} %copy-done.4, f32[2048]{0:T(1024)S(1)} %add_rsqrt_fusion, f32[2048]{0:T(1024)S(1)} %broadcast_multiply_fusion), kind=kOutput, calls=%fused_computation.28 | convolution fusion | flops 3242983424 | bytes 11558912 | tf_op jit(solution)/shard_map/dot_general | solution.py:72
  141.1 2.8 copy.55
  143.9 5.8 %all-to-all-start = ((bf16[2,1024,1,384]{3,0,2,1:T(2,128)(2,1)}), bf16[2,1024,1,384]{3,0,2,1:T(2,128)(2,1)}, u32[]{:S(2)}, u32[]{:S(2)}) async-start(bf16[2,1024,1,384]{3,0,2,1:T(2,128)(2,1)} %copy.55), calls=%async_computation | async-start | bytes 3145728 | tf_op jit(solution)/shard_map/all_to_all | solution.py:79
  149.7 27.8 %all-to-all-done = bf16[2,1024,1,384]{3,0,2,1:T(2,128)(2,1)} async-done(((bf16[2,1024,1,384]{3,0,2,1:T(2,128)(2,1)}), bf16[2,1024,1,384]{3,0,2,1:T(2,128)(2,1)}, u32[]{:S(2)}, u32[]{:S(2)}) %all-to-all-start) | async-done | bytes 1572896 | tf_op jit(solution)/shard_map/all_to_all | solution.py:79
  177.4 2.5 copy.84
  179.9 1.5 all_to_all.55
  181.5 1.6 fusion.29
  183.1 0.8 copy.57
  186.5 7.8 %all-to-all-start.3 = ((f32[16,1,128]{2,1,0:T(1,128)}), f32[16,1,128]{2,1,0:T(1,128)S(1)}, u32[]{:S(2)}, u32[]{:S(2)}) async-start(f32[16,1,128]{2,1,0:T(1,128)} %reshape.99), calls=%async_computation.3 | async-start | bytes 16384 | tf_op jit(solution)/shard_map/all_to_all | solution.py:58
  196.8 6.5 %all-to-all-done.3 = f32[16,1,128]{2,1,0:T(1,128)S(1)} async-done(((f32[16,1,128]{2,1,0:T(1,128)}), f32[16,1,128]{2,1,0:T(1,128)S(1)}, u32[]{:S(2)}, u32[]{:S(2)}) %all-to-all-start.3) | async-done | bytes 8224 | tf_op jit(solution)/shard_map/all_to_all | solution.py:58
  203.2 3.5 %all-to-all-start.1 = ((f32[16,1,128]{2,1,0:T(1,128)}), f32[16,1,128]{2,1,0:T(1,128)S(1)}, u32[]{:S(2)}, u32[]{:S(2)}) async-start(f32[16,1,128]{2,1,0:T(1,128)} %reshape.101), calls=%async_computation.1 | async-start | bytes 16384 | tf_op jit(solution)/shard_map/all_to_all | solution.py:57
  206.7 1.3 convolution_bitcast_fusion
  208.0 1.6 copy.66
  209.7 5.8 %all-to-all-done.1 = f32[16,1,128]{2,1,0:T(1,128)S(1)} async-done(((f32[16,1,128]{2,1,0:T(1,128)}), f32[16,1,128]{2,1,0:T(1,128)S(1)}, u32[]{:S(2)}, u32[]{:S(2)}) %all-to-all-start.1) | async-done | bytes 8224 | tf_op jit(solution)/shard_map/all_to_all | solution.py:57
  215.4 4.4 %all-to-all-start.2 = ((f32[32,64,1,128]{3,1,2,0:T(8,128)}), f32[32,64,1,128]{3,1,2,0:T(8,128)}, u32[]{:S(2)}, u32[]{:S(2)}) async-start(f32[32,64,1,128]{3,1,2,0:T(8,128)} %copy.66), calls=%async_computation.2 | async-start | bytes 2097152 | tf_op jit(solution)/shard_map/all_to_all | solution.py:56
  219.8 14.5 %while.14 = (s32[]{:T(128)}, f32[2,1024,1,128]{3,1,0,2:T(8,128)}, f32[2,1024,1]{1,0,2:T(2,128)S(1)}, f32[2,1024,1]{1,0,2:T(2,128)S(1)}, bf16[2,1024,1,384]{3,1,2,0:T(8,128)(2,1)S(1)}, /*index=5*/s32[]{:T(128)}, s32[]{:T(128)}) while((s32[]{:T(128)}, f32[2,1024,1,128]{3,1,0,2:T(8,128)}, f32[2,1024,1]{1,0,2:T(2,128)S(1)}, ...), condition=%wide.region_5.6_spmd, body=%wide.region_2.5_spmd.sunk | while | flops 553646080 | bytes 34374260 | solution.py:77
  220.7 1.9 copy-done
  223.5 0.8 constant_dynamic-update-slice_fusion.2
  224.3 2.7 fusion.48
  227.9 1.9 copy-done
  230.7 0.9 constant_dynamic-update-slice_fusion.2
  231.6 2.7 fusion.48
  236.3 1.3 copy.67
  237.6 2.8 fusion.28
  240.4 43.8 %all_gather.15 = bf16[2048,128]{1,0:T(8,128)(2,1)S(1)} all-gather(bf16[128,128]{1,0:T(8,128)(2,1)S(1)} %copy-done.3), channel_id=1, replica_groups=mesh['row'=16,'col'=16] {'row'}, dimensions={0}, use_global_device_ids=true | all-gather | bytes 557056 | tf_op jit(solution)/shard_map/all_gather | solution.py:71
  284.1 41.0 %all-gather.8.cloned.1.call-done = bf16[2048,2048]{1,0:T(8,128)(2,1)} async-done(((bf16[2048,128]{1,0:T(8,128)(2,1)}), bf16[2048,2048]{1,0:T(8,128)(2,1)}) %all-gather.8.cloned.1.call-update) | async-done | bytes 8388624 | tf_op jit(solution)/shard_map/all_gather | solution.py:91
  325.1 6.5 %fusion.25 = bf16[2048,128]{1,0:T(8,128)(2,1)} fusion(bf16[2048,2048]{1,0:T(8,128)(2,1)} %all-gather.8.cloned.1.call-done, bf16[2048,128]{1,0:T(8,128)(2,1)S(1)} %all_gather.15, bf16[2048,128]{1,0:T(8,128)(2,1)S(1)} %copy-done.2), kind=kOutput, calls=%fused_computation.30 | convolution fusion | flops 1074528256 | bytes 9961472 | tf_op jit(solution)/shard_map/dot_general | solution.py:90
  (55 shorter events, 11.9 us)
Async XLA Ops:
  6.5 70.5 %all-gather.4.cloned.1.call-start = ((), (), s32[]{:S(2)}) async-start(), calls=%async_computation.4 | async-start | bytes 8912896 | tf_op jit(solution)/shard_map/all_gather | solution.py:64
  7.3 125.4 %all-gather.6.cloned.1.call-start = ((), (), s32[]{:S(2)}) async-start(), calls=%async_computation.5 | async-start | bytes 1671168 | tf_op jit(solution)/shard_map/all_gather | solution.py:70
  77.0 5.8 %copy-start.1 = (bf16[2048,2048]{1,0:T(8,128)(2,1)S(1)}, bf16[2048,2048]{1,0:T(8,128)(2,1)}, u32[]{:S(2)}) copy-start(bf16[2048,2048]{1,0:T(8,128)(2,1)} %all-gather.4.cloned.1.call-done) | copy-start | bytes 25165828
  82.8 49.9 %copy-start.4 = (f32[2048]{0:T(1024)S(1)}, f32[2048]{0:T(1024)}, u32[]{:S(2)}) copy-start(f32[2048]{0:T(1024)} %param.7) | copy-start | bytes 24580
  143.9 33.6 %all-to-all-start = ((bf16[2,1024,1,384]{3,0,2,1:T(2,128)(2,1)}), bf16[2,1024,1,384]{3,0,2,1:T(2,128)(2,1)}, u32[]{:S(2)}, u32[]{:S(2)}) async-start(bf16[2,1024,1,384]{3,0,2,1:T(2,128)(2,1)} %copy.55), calls=%async_computation | async-start | bytes 3145728 | tf_op jit(solution)/shard_map/all_to_all | solution.py:79
  186.5 16.7 %all-to-all-start.3 = ((f32[16,1,128]{2,1,0:T(1,128)}), f32[16,1,128]{2,1,0:T(1,128)S(1)}, u32[]{:S(2)}, u32[]{:S(2)}) async-start(f32[16,1,128]{2,1,0:T(1,128)} %reshape.99), calls=%async_computation.3 | async-start | bytes 16384 | tf_op jit(solution)/shard_map/all_to_all | solution.py:58
  203.2 12.2 %all-to-all-start.1 = ((f32[16,1,128]{2,1,0:T(1,128)}), f32[16,1,128]{2,1,0:T(1,128)S(1)}, u32[]{:S(2)}, u32[]{:S(2)}) async-start(f32[16,1,128]{2,1,0:T(1,128)} %reshape.101), calls=%async_computation.1 | async-start | bytes 16384 | tf_op jit(solution)/shard_map/all_to_all | solution.py:57
  215.4 20.8 %all-to-all-start.2 = ((f32[32,64,1,128]{3,1,2,0:T(8,128)}), f32[32,64,1,128]{3,1,2,0:T(8,128)}, u32[]{:S(2)}, u32[]{:S(2)}) async-start(f32[32,64,1,128]{3,1,2,0:T(8,128)} %copy.66), calls=%async_computation.2 | async-start | bytes 2097152 | tf_op jit(solution)/shard_map/all_to_all | solution.py:56
  219.8 105.3 %all-gather.8.cloned.1.call-start = ((), (), s32[]{:S(2)}) async-start(), calls=%async_computation.6 | async-start | bytes 8912896 | tf_op jit(solution)/shard_map/all_gather | solution.py:91
  220.7 1.9 copy-start
  227.9 1.9 copy-start
  234.4 6.0 %copy-start.3 = (bf16[128,128]{1,0:T(8,128)(2,1)S(1)}, bf16[128,128]{1,0:T(8,128)(2,1)}, u32[]{:S(2)}) copy-start(bf16[128,128]{1,0:T(8,128)(2,1)} %param.9) | copy-start | bytes 98308
  234.4 90.7 %copy-start.2 = (bf16[2048,128]{1,0:T(8,128)(2,1)S(1)}, bf16[2048,128]{1,0:T(8,128)(2,1)}, u32[]{:S(2)}) copy-start(bf16[2048,128]{1,0:T(8,128)(2,1)} %param.6) | copy-start | bytes 1572868
Sparse Core Ops, SparseCore 0:
  9.1 67.8 all-gather.3
  79.4 53.1 all-gather.5
  240.5 84.5 all-gather.7
where the time goes:
time: 339 us; the launch traced here: 338 us
  waiting for transfers between devices  199 us (59%)
  blocking collectives  43.8 us (13%)
  starting transfers between devices  21.5 us (6%)
  local copies, waits for them, and re-layouts  21.3 us (6%)
  matrix products  20.6 us (6%)
  other arithmetic  18.6 us (5%)
  between operations  13.3 us (4%)
    all_gather x1, waiting for transfers between devices, per_device(): gathered = lax.all_gather(signal, 'col', axis=1, tiled=True)  69 us
    all_gather x1, waiting for transfers between devices, per_device(): piece_qkv = lax.all_gather(qkv_weight, 'row', axis=0, tiled=True)  47.5 us
    all_gather x1, blocking collectives, per_device(): piece_out = lax.all_gather(out_weight, 'row', axis=0, tiled=True)  43.8 us
    all_gather x1, waiting for transfers between devices, per_device(): lax.all_gather(attended, 'col', axis=1, tiled=True)  41 us
    all_to_all x1, waiting for transfers between devices, per_device(): lax.all_to_all(stacked, 'row', split_axis=1, concat_axis=0, tiled=True)  27.8 us
    dot_general x1, matrix products, per_device(): jnp.dot(normed, piece_qkv, preferred_element_type=jnp.float32)  8.46 us
    all_to_all x1, starting transfers between devices, column_softmax(): lax.all_to_all(totals_rows, 'row', split_axis=0, concat_axis=1, tiled=True)  7.84 us
  transfers between devices with their start and end apart: 7, of which 6 were waited for; matrix products, arithmetic and copies ran while one was open for 7% of the time, Pallas kernels for 0%

commit v1 on v0

--- a/solution.py
+++ b/solution.py
@@ -8,6 +8,13 @@
 COLS = 1024
 EPSILON = 1e-05
 NEGATIVE = -1e30
+
+
+def all_by_exchange(block, axis, along):
+    size = lax.axis_size(axis)
+    blocks = jnp.stack([block for _ in range(size)])
+    blocks = lax.all_to_all(blocks, axis, split_axis=0, concat_axis=0)
+    return jnp.concatenate(blocks, axis=along)
 
 
 def row_softmax(row_block):
@@ -61,7 +68,7 @@
 
 def per_device(signal, norm_gain, qkv_weight, out_weight):
     samples = signal.shape[0]
-    gathered = lax.all_gather(signal, "col", axis=1, tiled=True)
+    gathered = all_by_exchange(signal, "col", 1)
     widened = gathered.astype(jnp.float32)
     average = jnp.mean(widened, axis=1, keepdims=True)
     variance = jnp.mean((widened - average) ** 2, axis=1, keepdims=True)

time: 339 us -> 393 us (1.16)
  waiting for transfers between devices: 199 us -> 220 us
  starting transfers between devices: 21.5 us -> 37.3 us
  other arithmetic: 18.6 us -> 33.1 us
  local copies, waits for them, and re-layouts: 21.3 us -> 30.4 us
  blocking collectives: 43.8 us -> 37.8 us
    all_to_all x0 -> x1, waiting for transfers between devices: none -> 123 us  [all_by_exchange(): blocks = lax.all_to_all(blocks, axis, split_axis=0, concat_axis=0)]
    all_gather x1 -> x0, waiting for transfers between devices: 69 us -> none  [per_device(): gathered = lax.all_gather(signal, 'col', axis=1, tiled=True)]
    all_gather x1, waiting for transfers between devices: 47.5 us -> 0.01 us  [per_device(): piece_qkv = lax.all_gather(qkv_weight, 'row', axis=0, tiled=True)]
    all_to_all x1, waiting for transfers between devices: 27.8 us -> 39.6 us  [per_device(): lax.all_to_all(stacked, 'row', split_axis=1, concat_axis=0, tiled=True)]
    all_to_all x1, starting transfers between devices: 5.78 us -> 15.6 us  [per_device(): lax.all_to_all(stacked, 'row', split_axis=1, concat_axis=0, tiled=True)]
    convert_element_type x0 -> x1, other arithmetic: none -> 9.07 us  [per_device(): ((widened - average) * lax.rsqrt(variance + EPSILON) * norm_gain).astype(...]
    all_to_all x0 -> x1, starting transfers between devices: none -> 7.67 us  [all_by_exchange(): blocks = lax.all_to_all(blocks, axis, split_axis=0, concat_axis=0)]
    all_gather x1, blocking collectives: 43.8 us -> 37.8 us  [per_device(): piece_out = lax.all_gather(out_weight, 'row', axis=0, tiled=True)]
  transfers between devices with their start and end apart: 7 -> 7, of which waited for: 6 -> 6; matrix products, arithmetic and copies ran while one was open for 7% -> 10% of each run, Pallas kernels for 0% -> 0%
where the time goes in v1:
time: 393 us; the launch traced here: 392 us
  waiting for transfers between devices  220 us (56%)
  blocking collectives  37.8 us (10%)
  starting transfers between devices  37.3 us (9%)
  other arithmetic  33.1 us (8%)
  local copies, waits for them, and re-layouts  30.4 us (8%)
  matrix products  20.4 us (5%)
  between operations  13.6 us (3%)
    all_to_all x1, waiting for transfers between devices, all_by_exchange(): blocks = lax.all_to_all(blocks, axis, split_axis=0, concat_axis=0)  123 us
    all_gather x1, waiting for transfers between devices, per_device(): lax.all_gather(attended, 'col', axis=1, tiled=True)  41 us
    all_to_all x1, waiting for transfers between devices, per_device(): lax.all_to_all(stacked, 'row', split_axis=1, concat_axis=0, tiled=True)  39.6 us
    all_gather x1, blocking collectives, per_device(): piece_out = lax.all_gather(out_weight, 'row', axis=0, tiled=True)  37.8 us
    all_to_all x1, starting transfers between devices, per_device(): lax.all_to_all(stacked, 'row', split_axis=1, concat_axis=0, tiled=True)  15.6 us
    convert_element_type x1, other arithmetic, per_device(): ((widened - average) * lax.rsqrt(variance + EPSILON) * norm_gain).astype(...  9.07 us
    dot_general x1, matrix products, per_device(): jnp.dot(normed, piece_qkv, preferred_element_type=jnp.float32)  8.36 us
  transfers between devices with their start and end apart: 7, of which 6 were waited for; matrix products, arithmetic and copies ran while one was open for 10% of the time, Pallas kernels for 0%

profile of v1, /device:TPU:1, one launch (start us, length us, event | category | flops | bytes accessed | tf_op | source)
XLA Modules:
  0.0 392.3 jit_solution(18243611229706872594)
XLA Ops:
  7.8 4.3 %stack.2 = bf16[16,2048,128]{1,2,0:T(8,128)(2,1)} broadcast(bf16[2048,128]{0,1:T(8,128)(2,1)S(1)} %copy.58), dimensions={1,2} | broadcast | bytes 8912896 | tf_op jit(solution)/shard_map/stack | solution.py:15
  12.1 7.7 %all-to-all-start = ((bf16[16,2048,128]{1,2,0:T(8,128)(2,1)}), bf16[16,2048,128]{1,2,0:T(8,128)(2,1)}, u32[]{:S(2)}, u32[]{:S(2)}) async-start(bf16[16,2048,128]{1,2,0:T(8,128)(2,1)} %stack.2), calls=%async_computation | async-start | bytes 16777216 | tf_op jit(solution)/shard_map/all_to_all | solution.py:16
  20.5 122.6 %all-to-all-done = bf16[16,2048,128]{1,2,0:T(8,128)(2,1)} async-done(((bf16[16,2048,128]{1,2,0:T(8,128)(2,1)}), bf16[16,2048,128]{1,2,0:T(8,128)(2,1)}, u32[]{:S(2)}, u32[]{:S(2)}) %all-to-all-start) | async-done | bytes 8388640 | tf_op jit(solution)/shard_map/all_to_all | solution.py:16
  143.1 4.7 %convert_reduce_fusion = f32[2048]{0:T(1024)S(1)} fusion(bf16[16,2048,128]{1,2,0:T(8,128)(2,1)} %all-to-all-done), kind=kLoop, calls=%fused_computation.22 | loop fusion | flops 8386560 | bytes 8396800 | tf_op jit(solution)/shard_map/reduce_sum | solution.py:73
  147.8 5.6 %multiply_reduce_fusion = f32[2048]{0:T(1024)S(1)} fusion(bf16[16,2048,128]{1,2,0:T(8,128)(2,1)} %all-to-all-done, f32[2048]{0:T(1024)S(1)} %broadcast_multiply_fusion), kind=kLoop, calls=%fused_computation.21 | loop fusion | flops 16775168 | bytes 8404992 | tf_op jit(solution)/shard_map/reduce_sum | solution.py:74
  153.4 9.1 %fusion.14 = bf16[2048,2048]{0,1:T(8,128)(2,1)} fusion(bf16[16,2048,128]{1,2,0:T(8,128)(2,1)} %all-to-all-done, f32[2048]{0:T(1024)S(1)} %copy-done.3, f32[2048]{0:T(1024)S(1)} %add_rsqrt_fusion, f32[2048]{0:T(1024)S(1)} %broadcast_multiply_fusion), kind=kLoop, calls=%fused_computation.20 | loop fusion | flops 20971520 | bytes 16801792 | tf_op jit(solution)/shard_map/convert_element_type | solution.py:75
  162.5 8.4 %convolution_convert_fusion = bf16[2048,384]{1,0:T(8,128)(2,1)S(1)} fusion(bf16[2048,2048]{0,1:T(8,128)(2,1)} %fusion.14, bf16[2048,384]{1,0:T(8,128)(2,1)} %all-gather.3.cloned.1.call-done), kind=kOutput, calls=%fused_computation.23 | convolution fusion | flops 3222011904 | bytes 11534336 | tf_op jit(solution)/shard_map/dot_general | solution.py:79
  170.9 3.0 copy.60
  173.8 15.6 %all-to-all-start.1 = ((bf16[2,1024,1,384]{3,0,2,1:T(2,128)(2,1)}), bf16[2,1024,1,384]{3,0,2,1:T(2,128)(2,1)S(1)}, u32[]{:S(2)}, u32[]{:S(2)}) async-start(bf16[2,1024,1,384]{3,0,2,1:T(2,128)(2,1)} %copy.60), calls=%async_computation.1 | async-start | bytes 3145728 | tf_op jit(solution)/shard_map/all_to_all | solution.py:86
  189.5 39.6 %all-to-all-done.1 = bf16[2,1024,1,384]{3,0,2,1:T(2,128)(2,1)S(1)} async-done(((bf16[2,1024,1,384]{3,0,2,1:T(2,128)(2,1)}), bf16[2,1024,1,384]{3,0,2,1:T(2,128)(2,1)S(1)}, u32[]{:S(2)}, u32[]{:S(2)}) %all-to-all-start.1) | async-done | bytes 1572896 | tf_op jit(solution)/shard_map/all_to_all | solution.py:86
  229.1 2.2 copy.89
  231.4 3.7 all_to_all.59
  235.0 1.4 fusion.19
  236.4 2.7 copy.62
  240.4 1.3 fusion.21
  243.9 6.2 %all-to-all-start.4 = ((f32[16,1,128]{2,1,0:T(1,128)}), f32[16,1,128]{2,1,0:T(1,128)S(1)}, u32[]{:S(2)}, u32[]{:S(2)}) async-start(f32[16,1,128]{2,1,0:T(1,128)} %reshape.111), calls=%async_computation.4 | async-start | bytes 16384 | tf_op jit(solution)/shard_map/all_to_all | solution.py:65
  251.7 1.5 copy.70
  253.2 5.7 %all-to-all-done.4 = f32[16,1,128]{2,1,0:T(1,128)S(1)} async-done(((f32[16,1,128]{2,1,0:T(1,128)}), f32[16,1,128]{2,1,0:T(1,128)S(1)}, u32[]{:S(2)}, u32[]{:S(2)}) %all-to-all-start.4) | async-done | bytes 8224 | tf_op jit(solution)/shard_map/all_to_all | solution.py:65
  258.9 3.4 all-to-all-start.2
  263.7 1.6 copy.71
  265.3 5.9 %all-to-all-done.2 = f32[16,1,128]{2,1,0:T(1,128)S(1)} async-done(((f32[16,1,128]{2,1,0:T(1,128)}), f32[16,1,128]{2,1,0:T(1,128)S(1)}, u32[]{:S(2)}, u32[]{:S(2)}) %all-to-all-start.2) | async-done | bytes 8224 | tf_op jit(solution)/shard_map/all_to_all | solution.py:64
  271.1 4.3 %all-to-all-start.3 = ((f32[32,64,1,128]{3,1,2,0:T(8,128)}), f32[32,64,1,128]{3,1,2,0:T(8,128)}, u32[]{:S(2)}, u32[]{:S(2)}) async-start(f32[32,64,1,128]{3,1,2,0:T(8,128)} %copy.71), calls=%async_computation.3 | async-start | bytes 2097152 | tf_op jit(solution)/shard_map/all_to_all | solution.py:63
  275.5 14.5 %while.14 = (s32[]{:T(128)}, f32[2,1024,1,128]{3,1,0,2:T(8,128)}, f32[2,1024,1]{1,0,2:T(2,128)S(1)}, f32[2,1024,1]{1,0,2:T(2,128)S(1)}, bf16[2,1024,1,384]{3,1,2,0:T(8,128)(2,1)S(1)}, /*index=5*/s32[]{:T(128)}, s32[]{:T(128)}) while((s32[]{:T(128)}, f32[2,1024,1,128]{3,1,0,2:T(8,128)}, f32[2,1024,1]{1,0,2:T(2,128)S(1)}, ...), condition=%wide.region_5.6_spmd, body=%wide.region_2.5_spmd.sunk | while | flops 553646080 | bytes 34374260 | solution.py:84
  276.4 1.9 copy-done
  280.0 2.7 fusion.39
  283.6 1.9 copy-done
  287.3 2.7 fusion.39
  292.0 4.0 %all-to-all-done.3 = f32[32,64,1,128]{3,1,2,0:T(8,128)} async-done(((f32[32,64,1,128]{3,1,2,0:T(8,128)}), f32[32,64,1,128]{3,1,2,0:T(8,128)}, u32[]{:S(2)}, u32[]{:S(2)}) %all-to-all-start.3) | async-done | bytes 1048608 | tf_op jit(solution)/shard_map/all_to_all | solution.py:63
  297.3 2.8 fusion.18
  300.1 37.8 %all_gather.11 = bf16[2048,128]{1,0:T(8,128)(2,1)S(1)} all-gather(bf16[128,128]{1,0:T(8,128)(2,1)S(1)} %copy-done.2), channel_id=1, replica_groups=mesh['row'=16,'col'=16] {'row'}, dimensions={0}, use_global_device_ids=true | all-gather | bytes 557056 | tf_op jit(solution)/shard_map/all_gather | solution.py:78
  337.9 41.0 %all-gather.5.cloned.1.call-done = bf16[2048,2048]{1,0:T(8,128)(2,1)} async-done(((bf16[2048,128]{1,0:T(8,128)(2,1)}), bf16[2048,2048]{1,0:T(8,128)(2,1)}) %all-gather.5.cloned.1.call-update) | async-done | bytes 8388624 | tf_op jit(solution)/shard_map/all_gather | solution.py:98
  378.9 6.5 %fusion.15 = bf16[2048,128]{1,0:T(8,128)(2,1)} fusion(bf16[2048,2048]{1,0:T(8,128)(2,1)} %all-gather.5.cloned.1.call-done, bf16[2048,128]{1,0:T(8,128)(2,1)S(1)} %all_gather.11, bf16[2048,128]{1,0:T(8,128)(2,1)S(1)} %copy-done.1), kind=kOutput, calls=%fused_computation.25 | convolution fusion | flops 1074528256 | bytes 9961472 | tf_op jit(solution)/shard_map/dot_general | solution.py:97
  (55 shorter events, 16.8 us)
Async XLA Ops:
  12.1 131.0 %all-to-all-start = ((bf16[16,2048,128]{1,2,0:T(8,128)(2,1)}), bf16[16,2048,128]{1,2,0:T(8,128)(2,1)}, u32[]{:S(2)}, u32[]{:S(2)}) async-start(bf16[16,2048,128]{1,2,0:T(8,128)(2,1)} %stack.2), calls=%async_computation | async-start | bytes 16777216 | tf_op jit(solution)/shard_map/all_to_all | solution.py:16
  19.7 142.8 %all-gather.3.cloned.1.call-start = ((), (), s32[]{:S(2)}) async-start(), calls=%async_computation.5 | async-start | bytes 1671168 | tf_op jit(solution)/shard_map/all_gather | solution.py:77
  147.8 5.6 %copy-start.3 = (f32[2048]{0:T(1024)S(1)}, f32[2048]{0:T(1024)}, u32[]{:S(2)}) copy-start(f32[2048]{0:T(1024)} %param.7) | copy-start | bytes 24580
  173.8 55.3 %all-to-all-start.1 = ((bf16[2,1024,1,384]{3,0,2,1:T(2,128)(2,1)}), bf16[2,1024,1,384]{3,0,2,1:T(2,128)(2,1)S(1)}, u32[]{:S(2)}, u32[]{:S(2)}) async-start(bf16[2,1024,1,384]{3,0,2,1:T(2,128)(2,1)} %copy.60), calls=%async_computation.1 | async-start | bytes 3145728 | tf_op jit(solution)/shard_map/all_to_all | solution.py:86
  243.9 15.0 %all-to-all-start.4 = ((f32[16,1,128]{2,1,0:T(1,128)}), f32[16,1,128]{2,1,0:T(1,128)S(1)}, u32[]{:S(2)}, u32[]{:S(2)}) async-start(f32[16,1,128]{2,1,0:T(1,128)} %reshape.111), calls=%async_computation.4 | async-start | bytes 16384 | tf_op jit(solution)/shard_map/all_to_all | solution.py:65
  258.9 12.2 %all-to-all-start.2 = ((f32[16,1,128]{2,1,0:T(1,128)}), f32[16,1,128]{2,1,0:T(1,128)S(1)}, u32[]{:S(2)}, u32[]{:S(2)}) async-start(f32[16,1,128]{2,1,0:T(1,128)} %reshape.113), calls=%async_computation.2 | async-start | bytes 16384 | tf_op jit(solution)/shard_map/all_to_all | solution.py:64
  271.1 24.8 %all-to-all-start.3 = ((f32[32,64,1,128]{3,1,2,0:T(8,128)}), f32[32,64,1,128]{3,1,2,0:T(8,128)}, u32[]{:S(2)}, u32[]{:S(2)}) async-start(f32[32,64,1,128]{3,1,2,0:T(8,128)} %copy.71), calls=%async_computation.3 | async-start | bytes 2097152 | tf_op jit(solution)/shard_map/all_to_all | solution.py:63
  275.5 103.4 %all-gather.5.cloned.1.call-start = ((), (), s32[]{:S(2)}) async-start(), calls=%async_computation.6 | async-start | bytes 8912896 | tf_op jit(solution)/shard_map/all_gather | solution.py:98
  276.4 1.9 copy-start
  283.6 1.9 copy-start
  290.1 10.0 %copy-start.2 = (bf16[128,128]{1,0:T(8,128)(2,1)S(1)}, bf16[128,128]{1,0:T(8,128)(2,1)}, u32[]{:S(2)}) copy-start(bf16[128,128]{1,0:T(8,128)(2,1)} %param.9) | copy-start | bytes 98308
  290.1 88.8 %copy-start.1 = (bf16[2048,128]{1,0:T(8,128)(2,1)S(1)}, bf16[2048,128]{1,0:T(8,128)(2,1)}, u32[]{:S(2)}) copy-start(bf16[2048,128]{1,0:T(8,128)(2,1)} %param.6) | copy-start | bytes 1572868
Sparse Core Ops, SparseCore 0:
  23.0 62.0 all-gather.2
  300.2 78.6 all-gather.4
